TPU v7x, 32 devices: a whole 2x2x4 slice. The times are simulated.
32 devices in a mesh: group: 2 (over x), lat: 16 (over z, y, core).
Axes of the slice: x: 2, y: 2, z: 4, core: 2. Of those that a mesh axis runs over, the one named last changes fastest.
Arguments:
- field: bfloat16 [1024, 512, 512], P(('group', 'lat')), parts along dimension 0, may hold values from -6 to 6
- lat_modes: float32 [64, 16, 16], replicated, may hold values from -1.5 to 1.5
- lat_gains: float32 [64, 16], replicated, may hold values from 2 to 16
- lat_local: float32 [16, 16], replicated, may hold values from -1.5 to 1.5
- depth_modes: float32 [16, 16, 16], replicated, may hold values from -1.5 to 1.5
- depth_local: float32 [16, 16], replicated, may hold values from -1.5 to 1.5
Outputs:
- result: bfloat16 [1024, 512, 512], P(('group', 'lat')), parts along dimension 0
There are 2 independent parts, one for each index of `group`. A program takes and returns all parts, laid end to end along the dimension named above; an argument that names none is the same for every part. Nothing has to cross between parts.
All inputs are finite; a program needn't handle non-finite values.
Results may differ from a plain program's by a relative error of at most 0.001.
Values may be sent and summed in bfloat16 or wider, within the bound.
A program may use at most 192 MiB of HBM per device.

v0:
```python
import math

import jax
import jax.numpy as jnp
from jax import lax
from jax.sharding import PartitionSpec as P


def cosine_basis(length, modes):
    order = jnp.arange(modes, dtype=jnp.float32)[:, None]
    place = jnp.arange(length, dtype=jnp.float32)[None, :]
    scales = jnp.where(order == 0.0, math.sqrt(1.0 / length), math.sqrt(2.0 / length))
    return jnp.cos(math.pi * order * (place + 0.5) / length) * scales


def row_tail(u_rows, spect, lat_local, depth_modes, depth_local, depth_basis):
    highest = lax.Precision.HIGHEST
    rows, width, cells = u_rows.shape
    chans = lat_local.shape[0]
    depth = cells // chans
    u4 = u_rows.reshape(rows, width, depth, chans)
    s4 = spect.reshape(rows, width, depth, chans)
    first = u4 + jax.nn.gelu(s4 + jnp.einsum("xyzc,cd->xyzd", u4, lat_local, precision=highest))
    dcoef = jnp.einsum("kz,xyzc->xykc", depth_basis, first, precision=highest)
    dmix = jnp.einsum("xykc,kcd->xykd", dcoef, depth_modes, precision=highest)
    dspect = jnp.einsum("kz,xykd->xyzd", depth_basis, dmix, precision=highest)
    final = first + jax.nn.gelu(
        dspect + jnp.einsum("xyzc,cd->xyzd", first, depth_local, precision=highest)
    )
    return final.reshape(rows, width, cells).astype(jnp.bfloat16)


def one_hot(ids, count):
    return (ids[:, None] == jnp.arange(count, dtype=jnp.int32)[None, :]).astype(jnp.float32)


def shards(field, lat_modes, lat_gains, lat_local, depth_modes, depth_local):
    highest = lax.Precision.HIGHEST
    devices = lax.axis_size("lat")
    rows_dev, width_y, cells = field.shape
    modes_x, chans, _ = lat_modes.shape
    modes_y = lat_gains.shape[0]
    modes_z = depth_modes.shape[0]
    depth = cells // chans
    width_x = rows_dev * devices
    basis_x = cosine_basis(width_x, modes_x)
    basis_y = cosine_basis(width_y, modes_y)
    basis_z = cosine_basis(depth, modes_z)
    start = lax.axis_index("lat")
    u_rows = field.astype(jnp.float32)
    coef_y = jnp.einsum("qy,xyw->xqw", basis_y, u_rows, precision=highest)
    packed = coef_y.reshape(rows_dev, modes_y * cells)
    gathered = lax.all_to_all(packed, "lat", split_axis=1, concat_axis=0, tiled=True)
    span = gathered.shape[1]
    pairs = span // chans
    coef = jnp.dot(basis_x, gathered, precision=highest).reshape(modes_x, pairs, chans)
    mode_ids = (start * pairs + jnp.arange(pairs, dtype=jnp.int32)) // depth
    gain_rows = jnp.dot(one_hot(mode_ids, modes_y), lat_gains, precision=highest)
    mixed = jnp.einsum("jpc,jcd->jpd", coef * gain_rows[None, :, :], lat_modes, precision=highest)
    back_x = jnp.dot(basis_x.T, mixed.reshape(modes_x, span), precision=highest)
    returned = lax.all_to_all(back_x, "lat", split_axis=0, concat_axis=1, tiled=True)
    spect = jnp.einsum(
        "qy,xqw->xyw", basis_y, returned.reshape(rows_dev, modes_y, cells), precision=highest
    )
    return row_tail(u_rows, spect, lat_local, depth_modes, depth_local, basis_z)


def solution(mesh):
    placed = (P(("group", "lat"), None, None), P(), P(), P(), P(), P())
    return jax.shard_map(
        shards,
        mesh=mesh,
        in_specs=placed,
        out_specs=P(("group", "lat"), None, None),
        check_vma=False,
    )
```

profile of v0, /device:TPU:13, one launch (start us, length us, event | category | flops | bytes accessed | tf_op | source)
XLA Modules:
  0.0 541.4 jit_solution(5286439165478162498)
XLA Ops:
  0.0 15.1 %convolution_bitcast_fusion = f32[32,64,512]{2,1,0:T(8,128)} fusion(bf16[32,512,512]{2,1,0:T(8,128)(2,1)} %param.6, f32[64]{0:T(128)S(1)} %get-tuple-element.5, f32[512]{0:T(512)S(1)} %iota_add_fusion, f32[64]{0:T(128)S(1)} %get-tuple-element.6), kind=kOutput, calls=%fused_computation.30 | convolution fusion | flops 6442549248 | bytes 20974080 | tf_op jit(solution)/shard_map/qy,xyw->xqw/dot_general | solution.py:51
  15.1 5.6 %all_to_all.24 = f32[32,16,2048]{2,1,0:T(8,128)} reshape(f32[32,64,512]{2,1,0:T(8,128)} %convolution_bitcast_fusion) | data formatting | bytes 8388608 | tf_op jit(solution)/shard_map/all_to_all | solution.py:53
  20.8 6.6 %copy.25 = f32[32,16,2048]{2,0,1:T(8,128)} copy(f32[32,16,2048]{2,1,0:T(8,128)} %all_to_all.24) | data formatting | bytes 8388608 | tf_op jit(solution)/shard_map/all_to_all | solution.py:53
  27.4 6.9 %all-to-all-start = ((f32[32,16,2048]{2,0,1:T(8,128)}), f32[32,16,2048]{2,0,1:T(8,128)}, u32[]{:S(2)}, u32[]{:S(2)}) async-start(f32[32,16,2048]{2,0,1:T(8,128)} %copy.25), calls=%async_computation | async-start | bytes 8388608 | tf_op jit(solution)/shard_map/all_to_all | solution.py:53
  34.3 0.3 copy.29
  34.7 0.2 fusion.62
  34.8 91.8 %all-to-all-done = f32[32,16,2048]{2,0,1:T(8,128)} async-done(((f32[32,16,2048]{2,0,1:T(8,128)}), f32[32,16,2048]{2,0,1:T(8,128)}, u32[]{:S(2)}, u32[]{:S(2)}) %all-to-all-start) | async-done | bytes 4194336 | tf_op jit(solution)/shard_map/all_to_all | solution.py:53
  126.6 5.3 copy.26
  131.9 8.9 %fusion.31 = f32[64,128,16]{1,0,2:T(8,128)S(1)} fusion(f32[128,16,512]{2,1,0:T(8,128)} %bitcast.60, f32[128,16]{0,1:T(8,128)S(1)} %fusion.62, f32[64]{0:T(128)S(1)} %get-tuple-element.5, f32[512]{0:T(512)S(1)} %iota_add_fusion, f32[64]{0:T(128)S(1)} %get-tuple-element.6), kind=kOutput, calls=%fused_computation.31 | convolution fusion | flops 805535744 | bytes 4729344 | tf_op jit(solution)/shard_map/dot_general | solution.py:56
  140.9 0.9 fusion.34
  141.8 0.6 copy.30
  142.4 6.9 %fusion.36 = f32[16,32,2048]{2,1,0:T(8,128)} fusion(f32[64,2048,1]{0,1,2:T(8,128)S(1)} %bitcast.61, f32[64]{0:T(128)S(1)} %get-tuple-element.5, f32[16,32]{1,0:T(8,128)S(1)} %add_add_fusion, f32[64]{0:T(128)S(1)} %get-tuple-element.6), kind=kOutput, calls=%fused_computation.34 | convolution fusion | flops 805404672 | bytes 4721152 | tf_op jit(solution)/shard_map/dot_general | solution.py:60
  149.3 5.3 all-to-all-start.1
  154.6 22.5 %copy.24 = bf16[32,512,512]{1,2,0:T(8,128)(2,1)} copy(bf16[32,512,512]{2,1,0:T(8,128)(2,1)} %param.6) | data formatting | bytes 33554432 | tf_op args[0]
  177.1 69.8 %all-to-all-done.1 = f32[16,32,2048]{2,1,0:T(8,128)} async-done(((f32[16,32,2048]{2,1,0:T(8,128)}), f32[16,32,2048]{2,1,0:T(8,128)}, u32[]{:S(2)}, u32[]{:S(2)}) %all-to-all-start.1) | async-done | bytes 4194336 | tf_op jit(solution)/shard_map/all_to_all | solution.py:61
  246.9 6.6 %copy.32 = f32[32,16,2048]{2,1,0:T(8,128)} copy(f32[32,16,2048]{2,0,1:T(8,128)} %bitcast.9) | data formatting | bytes 8388608 | tf_op jit(solution)/shard_map/all_to_all | solution.py:61
  253.5 5.2 reshape.105
  258.7 33.1 %fusion.42 = f32[32,512,512]{2,1,0:T(8,128)} fusion(f32[32,64,512]{2,1,0:T(8,128)} %reshape.105, f32[64]{0:T(128)S(1)} %get-tuple-element.5, f32[512]{0:T(512)S(1)} %iota_add_fusion, f32[64]{0:T(128)S(1)} %get-tuple-element.6), kind=kOutput, calls=%fused_computation.40 | convolution fusion | flops 6442549248 | bytes 37751296 | tf_op jit(solution)/shard_map/qy,xqw->xyw/dot_general | solution.py:62
  291.8 40.9 %fusion.7 = f32[32,512,32,16]{1,3,2,0:T(8,128)} fusion(f32[32,512,32,16]{1,3,2,0:T(8,128)} %bitcast.57, bf16[32,512,32,16]{1,3,2,0:T(8,128)(2,1)} %bitcast.58, f32[16,16]{1,0:T(8,128)S(1)} %copy-done.3), kind=kOutput, calls=%fused_computation.9 | convolution fusion | flops 1702887424 | bytes 83887104 | tf_op jit(solution)/shard_map/xyzc,cd->xyzd/dot_general | solution.py:23
  332.7 36.5 %fusion.26 = f32[32,512,16,16]{1,2,3,0:T(8,128)} fusion(f32[32,512,32,16]{1,3,2,0:T(8,128)} %fusion.7, f32[16]{0:T(128)S(1)} %get-tuple-element.7, f32[32]{0:T(128)S(1)} %iota_add_fusion.1, f32[16]{0:T(128)S(1)} %get-tuple-element.8), kind=kOutput, calls=%fused_computation.27 | convolution fusion | flops 1610614272 | bytes 50331904 | tf_op jit(solution)/shard_map/kz,xyzc->xykc/dot_general | solution.py:24
  369.2 37.9 %fusion.23 = f32[32,512,16,16]{1,3,0,2:T(8,128)} fusion(f32[32,512,16,16]{1,2,3,0:T(8,128)} %fusion.26, f32[16,16,16]{2,1,0:T(8,128)S(1)} %copy-done), kind=kOutput, calls=%fused_computation.26 | convolution fusion | flops 805306368 | bytes 33570816 | tf_op jit(solution)/shard_map/xykc,kcd->xykd/dot_general | solution.py:25
  407.1 42.6 %fusion.19 = f32[32,512,16,32]{1,3,2,0:T(8,128)} fusion(f32[32,512,16,16]{1,3,0,2:T(8,128)} %fusion.23, f32[16]{0:T(128)S(1)} %get-tuple-element.7, f32[32]{0:T(128)S(1)} %iota_add_fusion.1, f32[16]{0:T(128)S(1)} %get-tuple-element.8), kind=kOutput, calls=%fused_computation.22 | convolution fusion | flops 1610614272 | bytes 50331904 | tf_op jit(solution)/shard_map/kz,xykd->xyzd/dot_general | solution.py:26
  449.7 69.0 %fusion.16 = bf16[32,512,32,16]{1,3,2,0:T(8,128)(2,1)} fusion(f32[32,512,32,16]{1,3,2,0:T(8,128)} %fusion.7, f32[32,512,16,32]{1,3,2,0:T(8,128)} %fusion.19, f32[16,16]{1,0:T(8,128)S(1)} %copy-done.4), kind=kOutput, calls=%fused_computation.18 | convolution fusion | flops 1702887424 | bytes 83887104 | tf_op jit(solution)/shard_map/xyzc,cd->xyzd/dot_general | solution.py:28
  518.6 22.5 %copy.40 = bf16[32,512,512]{2,1,0:T(8,128)(2,1)} copy(bf16[32,512,512]{1,2,0:T(8,128)(2,1)} %bitcast.59) | data formatting | bytes 33554432 | tf_op jit(solution)/shard_map/convert_element_type | solution.py:30
  (16 shorter events, 0.1 us)
Async XLA Ops:
  0.0 369.2 %copy-start = (f32[16,16,16]{2,1,0:T(8,128)S(1)}, f32[16,16,16]{2,1,0:T(8,128)}, u32[]{:S(2)}) copy-start(f32[16,16,16]{2,1,0:T(8,128)} %param.10) | copy-start | bytes 49156
  0.0 34.3 %copy-start.1 = (f32[64,16,16]{0,2,1:T(8,128)S(1)}, f32[64,16,16]{0,2,1:T(8,128)}, u32[]{:S(2)}) copy-start(f32[64,16,16]{0,2,1:T(8,128)} %param.7) | copy-start | bytes 196612
  0.0 34.6 %copy-start.2 = (f32[64,16]{0,1:T(8,128)S(1)}, f32[64,16]{0,1:T(8,128)}, u32[]{:S(2)}) copy-start(f32[64,16]{0,1:T(8,128)} %param.8) | copy-start | bytes 12292
  27.4 99.2 %all-to-all-start = ((f32[32,16,2048]{2,0,1:T(8,128)}), f32[32,16,2048]{2,0,1:T(8,128)}, u32[]{:S(2)}, u32[]{:S(2)}) async-start(f32[32,16,2048]{2,0,1:T(8,128)} %copy.25), calls=%async_computation | async-start | bytes 8388608 | tf_op jit(solution)/shard_map/all_to_all | solution.py:53
  149.3 97.6 %all-to-all-start.1 = ((f32[16,32,2048]{2,1,0:T(8,128)}), f32[16,32,2048]{2,1,0:T(8,128)}, u32[]{:S(2)}, u32[]{:S(2)}) async-start(f32[16,32,2048]{2,1,0:T(8,128)} %fusion.36), calls=%async_computation.1 | async-start | bytes 8388608 | tf_op jit(solution)/shard_map/all_to_all | solution.py:61
  177.1 114.7 %copy-start.3 = (f32[16,16]{1,0:T(8,128)S(1)}, f32[16,16]{1,0:T(8,128)}, u32[]{:S(2)}) copy-start(f32[16,16]{1,0:T(8,128)} %param.9) | copy-start | bytes 3076
  407.1 42.6 %copy-start.4 = (f32[16,16]{1,0:T(8,128)S(1)}, f32[16,16]{1,0:T(8,128)}, u32[]{:S(2)}) copy-start(f32[16,16]{1,0:T(8,128)} %param.11) | copy-start | bytes 3076
where the time goes:
time: 548 us; the launch traced here: 541 us
  matrix products  292 us (53%)
  waiting for transfers between devices  162 us (30%)
  local copies, waits for them, and re-layouts  75.3 us (14%)
  starting transfers between devices  12.2 us (2%)
    all_to_all x1, waiting for transfers between devices, shards(): lax.all_to_all(packed, 'lat', split_axis=1, concat_axis=0, tiled=True)  91.8 us
    all_to_all x1, waiting for transfers between devices, shards(): lax.all_to_all(back_x, 'lat', split_axis=0, concat_axis=1, tiled=True)  69.8 us
    dot_general x1, matrix products, row_tail(): jnp.einsum('xyzc,cd->xyzd', first, depth_local, precision=highest)  69 us
    dot_general x1, matrix products, row_tail(): dspect = jnp.einsum('kz,xykd->xyzd', depth_basis, dmix, precision=highest)  42.6 us
    dot_general x1, matrix products, row_tail(): jnp.einsum('xyzc,cd->xyzd', u4, lat_local, precision=highest)  40.9 us
    dot_general x1, matrix products, row_tail(): dmix = jnp.einsum('xykc,kcd->xykd', dcoef, depth_modes, precision=highest)  37.9 us
    dot_general x1, matrix products, row_tail(): dcoef = jnp.einsum('kz,xyzc->xykc', depth_basis, first, precision=highest)  36.5 us
    dot_general x1, matrix products, shards(): jnp.einsum('qy,xqw->xyw', basis_y, returned.reshape(rows_dev, modes_y, ce...  33.1 us
  transfers between devices with their start and end apart: 2, of which 2 were waited for; matrix products, arithmetic and copies ran while one was open for 4% of the time, Pallas kernels for 0%

commit v1 on v0

v1 whole, which is shorter than its diff:
```python
import functools
import math

import jax
import jax.numpy as jnp
import numpy as np
from jax import lax
from jax.experimental import pallas as pl
from jax.experimental.pallas import tpu as pltpu
from jax.sharding import PartitionSpec as P

LINK = jnp.float16
SCALE_OUT = 256.0
SCALE_BACK = 1.0 / 16.0
K0 = math.sqrt(2.0 / math.pi)
K1 = K0 * 0.044715
MIB = 1 << 20


def cosine_basis(length, modes):
    order = np.arange(modes, dtype=np.float64)[:, None]
    place = np.arange(length, dtype=np.float64)[None, :]
    scales = np.where(order == 0.0, math.sqrt(1.0 / length), math.sqrt(2.0 / length))
    return (np.cos(math.pi * order * (place + 0.5) / length) * scales).astype(np.float32)


def halves(x):
    high = jnp.asarray(x).astype(jnp.bfloat16)
    low = (x - high.astype(jnp.float32)).astype(jnp.bfloat16)
    return high, low


def outer_halves(x):
    high = lax.reduce_precision(x, 8, 7)
    return high.astype(jnp.bfloat16), (x - high).astype(jnp.bfloat16)


def np_halves(x):
    high = np.asarray(x, dtype=jnp.bfloat16)
    low = np.asarray(x - high.astype(np.float32), dtype=jnp.bfloat16)
    return high, low


def dot(a, b):
    return jnp.dot(a, b, preferred_element_type=jnp.float32)


def gelu(x):
    half = 0.5 * x
    return half + half * jnp.tanh(x * (K0 + K1 * (x * x)))


def forward_kernel(basis_ref, u_ref, out_ref):
    modes = out_ref.shape[1]

    def body(row, carry):
        both = dot(basis_ref[...], u_ref[row])
        out_ref[row] = (both[:modes] + both[modes:]) * SCALE_OUT
        return carry

    lax.fori_loop(0, u_ref.shape[0], body, 0)


def forward(field, basis, start, rows):
    _, width, cells = field.shape
    modes = basis.shape[0] // 2
    step = math.gcd(rows, 4)
    return pl.pallas_call(
        forward_kernel,
        grid=(rows // step,),
        in_specs=[
            pl.BlockSpec(basis.shape, lambda i: (0, 0)),
            pl.BlockSpec((step, width, cells), lambda i: (i + start // step, 0, 0)),
        ],
        out_specs=pl.BlockSpec((step, modes, cells), lambda i: (i, 0, 0)),
        out_shape=jax.ShapeDtypeStruct((rows, modes, cells), jnp.float32),
        compiler_params=pltpu.CompilerParams(vmem_limit_bytes=40 * MIB),
        cost_estimate=pl.CostEstimate(
            flops=4 * rows * modes * width * cells,
            bytes_accessed=rows * cells * (2 * width + 4 * modes),
            transcendentals=0,
        ),
    )(basis, field)


def middle_kernel(chunks, chans, *refs):
    g_refs = refs[:chunks]
    f_refs = refs[chunks : 2 * chunks]
    b_refs = refs[2 * chunks : 3 * chunks]
    gain_ref, diag_ref = refs[3 * chunks : 3 * chunks + 2]
    out_refs = refs[3 * chunks + 2 :]
    modes = diag_ref.shape[1]
    coef = None
    for g_ref, f_ref in zip(g_refs, f_refs):
        high, low = halves(g_ref[0])
        both = dot(f_ref[...], high)
        part = both[:modes] + both[modes:] + dot(f_ref[:modes], low)
        coef = part if coef is None else coef + part
    coef = coef * gain_ref[0]
    tiles = []
    for lane in range(0, coef.shape[1], 128):
        tile = coef[:, lane : lane + 128]
        total = tile * diag_ref[chans - 1]
        for at in range(2 * chans - 1):
            shift = at - (chans - 1)
            if shift != 0:
                total += pltpu.roll(tile, (-shift) % 128, 1) * diag_ref[at]
        tiles.append(total)
    mixed = jnp.concatenate(tiles, axis=1) if len(tiles) > 1 else tiles[0]
    high, low = halves(mixed)
    stacked = jnp.concatenate([high, low, high], axis=0)
    for b_ref, out_ref in zip(b_refs, out_refs):
        out_ref[0] = dot(b_ref[...], stacked)


def middle(gathered, fronts, backs, gains, diags):
    chunks = len(gathered)
    count, length, width = gathered[0].shape
    modes = diags.shape[1]
    chans = (diags.shape[0] + 1) // 2
    whole = lambda a: pl.BlockSpec(a.shape, lambda i: (0,) * a.ndim)
    block = pl.BlockSpec((1, length, width), lambda i: (i, 0, 0))
    return pl.pallas_call(
        functools.partial(middle_kernel, chunks, chans),
        grid=(count,),
        in_specs=[block] * chunks
        + [whole(a) for a in fronts]
        + [whole(a) for a in backs]
        + [pl.BlockSpec((1, 1, width), lambda i: (i, 0, 0)), whole(diags)],
        out_specs=[block] * chunks,
        out_shape=[jax.ShapeDtypeStruct((count, length, width), jnp.float32)] * chunks,
        compiler_params=pltpu.CompilerParams(vmem_limit_bytes=40 * MIB),
    )(*gathered, *fronts, *backs, gains, diags)


def tail_kernel(piece, u_ref, back_ref, basis_ref, local_ref, depth_ref, *refs):
    out_ref = refs[-1]
    _, width, cells = u_ref.shape
    block = local_ref.shape[1]
    high, low = halves(back_ref[0])
    stacked = jnp.concatenate([high, low, high], axis=0)

    def body(at, carry):
        rows = pl.ds(pl.multiple_of(at * piece, piece), piece)
        u = u_ref[0, rows, :]
        spect = dot(basis_ref[rows, :], stacked)
        parts = []
        for lane in range(0, cells, block):
            tile = u[:, lane : lane + block]
            parts.append(dot(tile, local_ref[0]) + dot(tile, local_ref[1]))
        local = jnp.concatenate(parts, axis=1) if len(parts) > 1 else parts[0]
        first = u.astype(jnp.float32) + gelu(spect + local)
        high1, low1 = halves(first)
        mix = dot(high1, depth_ref[0]) + dot(low1, depth_ref[0]) + dot(high1, depth_ref[1])
        out_ref[0, rows, :] = (first + gelu(mix)).astype(out_ref.dtype)
        return carry

    lax.fori_loop(0, width // piece, body, 0)


def tail(field, back, basis, local, depth, previous, start):
    rows, modes, cells = back.shape
    width = field.shape[1]
    whole = lambda a: pl.BlockSpec(a.shape, lambda i: (0,) * a.ndim)
    operands = [field, back, basis, local, depth]
    specs = [
        pl.BlockSpec((1, width, cells), lambda i: (i + start, 0, 0)),
        pl.BlockSpec((1, modes, cells), lambda i: (i, 0, 0)),
        whole(basis),
        whole(local),
        whole(depth),
    ]
    aliases = {}
    if previous is not None:
        aliases = {len(operands): 0}
        operands.append(previous)
        specs.append(pl.BlockSpec(memory_space=pl.ANY))
    return pl.pallas_call(
        functools.partial(tail_kernel, math.gcd(width, 256)),
        grid=(rows,),
        in_specs=specs,
        out_specs=pl.BlockSpec((1, width, cells), lambda i: (i + start, 0, 0)),
        out_shape=jax.ShapeDtypeStruct(field.shape, jnp.bfloat16),
        input_output_aliases=aliases,
        compiler_params=pltpu.CompilerParams(vmem_limit_bytes=48 * MIB),
        cost_estimate=pl.CostEstimate(
            flops=2 * rows * width * cells * (4 * cells),
            bytes_accessed=4 * rows * width * cells,
            transcendentals=2 * rows * width * cells,
        ),
    )(*operands)


def block_diagonal(small, size):
    chans = small.shape[0]
    copies = size // chans
    ids = np.arange(size) // chans
    mask = (ids[:, None] == ids[None, :]).astype(np.float32)
    return jnp.tile(small, (copies, copies)) * mask


def shards(field, lat_modes, lat_gains, lat_local, depth_modes, depth_local):
    highest = lax.Precision.HIGHEST
    devices = lax.axis_size("lat")
    rows_dev, width_y, cells = field.shape
    modes_x, chans, _ = lat_modes.shape
    modes_y = lat_gains.shape[0]
    modes_z = depth_modes.shape[0]
    depth = cells // chans
    width_x = rows_dev * devices
    chunks = 2 if rows_dev % 16 == 0 else 1
    rows = rows_dev // chunks
    splits = max(1, devices // modes_y)
    held = modes_y * splits // devices
    span = cells // splits
    basis_x = cosine_basis(width_x, modes_x)
    basis_y = cosine_basis(width_y, modes_y)
    basis_z = cosine_basis(depth, modes_z)

    high_y, low_y = np_halves(basis_y)
    front_y = jnp.asarray(np.concatenate([high_y, low_y], axis=0))
    back_y = jnp.asarray(np.concatenate([high_y, high_y, low_y], axis=0).T.copy())
    fronts, backs = [], []
    for chunk in range(chunks):
        part = basis_x.reshape(modes_x, devices, chunks, rows)[:, :, chunk].reshape(modes_x, -1)
        high_x, low_x = np_halves(part)
        fronts.append(jnp.asarray(np.concatenate([high_x, low_x], axis=0)))
        backs.append(jnp.asarray(np.concatenate([high_x, high_x, low_x], axis=0).T.copy()))

    gathered = []
    for chunk in range(chunks):
        coef_y = forward(field, front_y, chunk * rows, rows)
        sent = coef_y.astype(LINK).reshape(rows, modes_y, splits, span)
        sent = sent.transpose(1, 2, 0, 3).reshape(modes_y * splits, rows, span)
        gathered.append(lax.all_to_all(sent, "lat", split_axis=0, concat_axis=0, tiled=True))

    shift = np.arange(2 * chans - 1)[:, None, None] - (chans - 1)
    places = np.arange(chans)
    pick = (places[None, :, None] == places[None, None, :] + shift).astype(np.float32)
    diags = jnp.sum(lat_modes[None] * pick[:, None], axis=2)
    diags = jnp.tile(diags, (1, 1, 128 // chans))
    me = lax.axis_index("lat")
    gain_rows = lax.dynamic_slice_in_dim(lat_gains, me * held // splits, held, 0)
    gain_rows = jnp.tile(gain_rows * (SCALE_BACK / SCALE_OUT), (1, span // chans))[:, None, :]

    spread = np.kron(basis_z.T, np.eye(chans, dtype=np.float32))
    ids = np.arange(modes_z * chans) // chans
    mask = (ids[:, None] == ids[None, :]).astype(np.float32)
    mixers = jnp.tile(depth_modes.reshape(modes_z * chans, chans), (1, modes_z)) * mask
    inner = jnp.dot(mixers, spread.T, precision=highest)
    whole = jnp.dot(spread, inner, precision=highest) + block_diagonal(depth_local, cells)
    depth_pair = jnp.stack(outer_halves(whole))
    local_pair = jnp.stack(outer_halves(block_diagonal(lat_local, math.gcd(cells, 256))))

    received = []
    for got in gathered:
        got = got.reshape(devices, held, rows, span).transpose(1, 0, 2, 3).astype(jnp.float32)
        received.append(got.reshape(held, devices * rows, span))
    mixed = middle(received, fronts, backs, gain_rows, diags)
    returned = []
    for part in mixed:
        part = part.astype(LINK).reshape(held, devices, rows, span).transpose(1, 0, 2, 3)
        part = part.reshape(devices * held, rows, span)
        returned.append(lax.all_to_all(part, "lat", split_axis=0, concat_axis=0, tiled=True))
    out = None
    for chunk, part in enumerate(returned):
        part = part.reshape(modes_y, splits, rows, span).transpose(2, 0, 1, 3)
        part = part.reshape(rows, modes_y, cells).astype(jnp.float32) * (1.0 / SCALE_BACK)
        out = tail(field, part, back_y, local_pair, depth_pair, out, chunk * rows)
    return out


def solution(mesh):
    placed = (P(("group", "lat"), None, None), P(), P(), P(), P(), P())
    return jax.shard_map(
        shards,
        mesh=mesh,
        in_specs=placed,
        out_specs=P(("group", "lat"), None, None),
        check_vma=False,
    )
```

time: 548 us -> 197 us (0.36)
  matrix products: 292 us -> 1.72 us
  waiting for transfers between devices: 162 us -> 38.2 us
  Pallas kernels: 0 us -> 94.6 us
  local copies, waits for them, and re-layouts: 75.3 us -> 19.8 us
  other arithmetic: 0.05 us -> 18.3 us
  starting transfers between devices: 12.2 us -> 21.6 us
    dot_general x11 -> x2, matrix products: 292 us -> 1.72 us  [the longest x1 1.08 us: shards(): jnp.dot(spread, inner, precision=highest)]
    all_to_all x2 -> x4, waiting for transfers between devices: 162 us -> 38.2 us  [the longest x2 37.6 us: shards(): lax.all_to_all(sent, 'lat', split_axis=0, concat_axis=0, tiled=True)]
    pallas_call x0 -> x5, Pallas kernels: none -> 94.6 us  [the longest x2 75 us: tail(): pl.pallas_call(functools.partial(tail_kernel, math.gcd(width, 256)), grid...]
    convert_element_type x1 -> x0, local copies, waits for them, and re-layouts: 22.5 us -> none  [row_tail(): return final.reshape(rows, width, cells).astype(jnp.bfloat16)]
    unnamed x12 -> x41, local copies, waits for them, and re-layouts: 22.8 us -> 3.7 us
    all_to_all x3 -> x0, local copies, waits for them, and re-layouts: 18.8 us -> none  [the longest x2 12.3 us: shards(): lax.all_to_all(packed, 'lat', split_axis=1, concat_axis=0, tiled=True)]
    mul x0 -> x6, other arithmetic: none -> 12.9 us  [the longest x2 10.3 us: block_diagonal(): return jnp.tile(small, (copies, copies)) * mask]
    all_to_all x2 -> x4, starting transfers between devices: 12.2 us -> 21.6 us  [the longest x2 11.3 us: shards(): lax.all_to_all(sent, 'lat', split_axis=0, concat_axis=0, tiled=True)]
  transfers between devices with their start and end apart: 2 -> 4, of which waited for: 2 -> 3; matrix products, arithmetic and copies ran while one was open for 4% -> 15% of each run, Pallas kernels for 0% -> 22%
where the time goes in v1:
time: 197 us; the launch traced here: 195 us
  Pallas kernels  94.6 us (48%)
  waiting for transfers between devices  38.2 us (19%)
  starting transfers between devices  21.6 us (11%)
  local copies, waits for them, and re-layouts  19.8 us (10%)
  other arithmetic  18.3 us (9%)
    pallas_call x2, Pallas kernels, tail(): pl.pallas_call(functools.partial(tail_kernel, math.gcd(width, 256)), grid...  75 us
    all_to_all x2, waiting for transfers between devices, shards(): lax.all_to_all(sent, 'lat', split_axis=0, concat_axis=0, tiled=True)  37.6 us
    pallas_call x2, Pallas kernels, forward(): pl.pallas_call(forward_kernel, grid=(rows // step,), in_specs=[pl.BlockSp...  12.4 us
    all_to_all x2, starting transfers between devices, shards(): lax.all_to_all(sent, 'lat', split_axis=0, concat_axis=0, tiled=True)  11.3 us
    mul x2, other arithmetic, block_diagonal(): return jnp.tile(small, (copies, copies)) * mask  10.3 us
    all_to_all x2, starting transfers between devices, shards(): lax.all_to_all(part, 'lat', split_axis=0, concat_axis=0, tiled=True)  10.2 us
    mul x2, local copies, waits for them, and re-layouts, block_diagonal(): return jnp.tile(small, (copies, copies)) * mask  8.61 us
    pallas_call x1, Pallas kernels, middle(): pl.pallas_call(functools.partial(middle_kernel, chunks, chans), grid=(cou...  7.19 us
  transfers between devices with their start and end apart: 4, of which 3 were waited for; matrix products, arithmetic and copies ran while one was open for 15% of the time, Pallas kernels for 22%

profile of v1, /device:TPU:13, one launch (start us, length us, event | category | flops | bytes accessed | tf_op | source)
XLA Modules:
  0.0 194.6 jit_solution(445326577981977641)
XLA Ops:
  0.9 6.2 %shard_map.173 = f32[16,64,512]{2,1,0:T(8,128)S(1)} custom-call(bf16[128,512]{1,0:T(8,128)(2,1)S(1)} %copy-done.4, bf16[32,512,512]{2,1,0:T(8,128)(2,1)} %u_ref.7), custom_call_target="tpu_custom_call" | custom-call | flops 1073741824 | bytes 10485760 | tf_op jit(solution)/shard_map/pallas_call | solution.py:68
  7.4 1.7 copy.62
  9.1 6.5 %all-to-all-start.1 = ((f16[64,16,512]{2,1,0:T(8,128)(2,1)}), f16[64,16,512]{2,1,0:T(8,128)(2,1)S(1)}, u32[]{:S(2)}, u32[]{:S(2)}) async-start(f16[64,16,512]{2,1,0:T(8,128)(2,1)} %copy.62), calls=%async_computation.1 | async-start | bytes 2097152 | tf_op jit(solution)/shard_map/all_to_all | solution.py:235
  15.6 6.2 %shard_map.172 = f32[16,64,512]{2,1,0:T(8,128)S(1)} custom-call(bf16[128,512]{1,0:T(8,128)(2,1)S(1)} %copy-done.5, bf16[32,512,512]{2,1,0:T(8,128)(2,1)} %u_ref.7), custom_call_target="tpu_custom_call" | custom-call | flops 1073741824 | bytes 10485760 | tf_op jit(solution)/shard_map/pallas_call | solution.py:68
  22.2 1.7 copy.60
  23.8 16.7 %all-to-all-done.1 = f16[64,16,512]{2,1,0:T(8,128)(2,1)S(1)} async-done(((f16[64,16,512]{2,1,0:T(8,128)(2,1)}), f16[64,16,512]{2,1,0:T(8,128)(2,1)S(1)}, u32[]{:S(2)}, u32[]{:S(2)}) %all-to-all-start.1) | async-done | bytes 1048608 | tf_op jit(solution)/shard_map/all_to_all | solution.py:235
  40.5 4.8 %all-to-all-start = ((f16[64,16,512]{2,1,0:T(8,128)(2,1)}), f16[64,16,512]{2,1,0:T(8,128)(2,1)}, u32[]{:S(2)}, u32[]{:S(2)}) async-start(f16[64,16,512]{2,1,0:T(8,128)(2,1)} %copy.60), calls=%async_computation | async-start | bytes 2097152 | tf_op jit(solution)/shard_map/all_to_all | solution.py:235
  45.7 1.2 multiply_reduce_fusion
  47.7 1.5 convert.7
  49.4 20.9 %all-to-all-done = f16[64,16,512]{2,1,0:T(8,128)(2,1)} async-done(((f16[64,16,512]{2,1,0:T(8,128)(2,1)}), f16[64,16,512]{2,1,0:T(8,128)(2,1)}, u32[]{:S(2)}, u32[]{:S(2)}) %all-to-all-start) | async-done | bytes 1048608 | tf_op jit(solution)/shard_map/all_to_all | solution.py:235
  70.3 1.5 convert.6
  72.8 7.2 %shard_map.174 = (f32[4,256,512]{2,1,0:T(8,128)S(1)}, f32[4,256,512]{2,1,0:T(8,128)S(1)}) custom-call(f32[4,256,512]{2,1,0:T(8,128)S(1)} %bitcast.62, f32[4,256,512]{2,1,0:T(8,128)S(1)} %bitcast.61, bf16[128,256]{1,0:T(8,128)(2,1)S(1)} %copy-done.9, bf16[128,256]{1,0:T(8,128)(2,1)S(1)} %copy-done.8, bf16[256,192]{1,0:T(8,128)(2,1)S(1)} %copy-done.7, ...), custom_call_target="tpu_custom_call" | custom-call | tf_op jit(solution)/shard_map/pallas_call | solution.py:123
  80.3 1.3 copy.70
  81.6 4.8 %all-to-all-start.3 = ((f16[64,16,512]{2,1,0:T(8,128)(2,1)}), f16[64,16,512]{2,1,0:T(8,128)(2,1)S(1)}, u32[]{:S(2)}, u32[]{:S(2)}) async-start(f16[64,16,512]{2,1,0:T(8,128)(2,1)} %bitcast.27), calls=%async_computation.3 | async-start | bytes 2097152 | tf_op jit(solution)/shard_map/all_to_all | solution.py:264
  86.5 1.8 broadcast_multiply_fusion.1
  89.3 8.4 %broadcast_multiply_fusion = f32[32,16,32,16]{3,2,1,0:T(8,128)} fusion(f32[32,16,32,16]{3,2,1,0:T(8,128)} %constant.63, f32[16,16]{1,0:T(8,128)S(1)} %copy-done.19), kind=kLoop, calls=%fused_computation | loop fusion | flops 262144 | bytes 2098176 | tf_op jit(solution)/shard_map/mul | solution.py:199
  97.7 7.7 %reshape.94 = f32[512,512]{1,0:T(8,128)S(1)} reshape(f32[32,16,32,16]{3,2,1,0:T(8,128)} %broadcast_multiply_fusion) | data formatting | bytes 2097152 | tf_op jit(solution)/shard_map/mul | solution.py:199
  106.4 1.1 fusion.2
  107.7 1.4 copy-done.3
  109.4 1.3 copy.67
  111.3 5.4 %all-to-all-start.2 = ((f16[64,16,512]{2,1,0:T(8,128)(2,1)}), f16[64,16,512]{2,1,0:T(8,128)(2,1)}, u32[]{:S(2)}, u32[]{:S(2)}) async-start(f16[64,16,512]{2,1,0:T(8,128)(2,1)} %bitcast.15), calls=%async_computation.2 | async-start | bytes 2097152 | tf_op jit(solution)/shard_map/all_to_all | solution.py:264
  117.6 37.5 %shard_map.175.refs_0_ = bf16[32,512,512]{2,1,0:T(8,128)(2,1)} custom-call(bf16[32,512,512]{2,1,0:T(8,128)(2,1)} %u_ref.7, f32[16,64,512]{2,1,0:T(8,128)S(1)} %multiply_bitcast_fusion.back_ref, bf16[512,192]{1,0:T(8,128)(2,1)S(1)} %copy-done.10, bf16[2,256,256]{2,1,0:T(8,128)(2,1)S(1)} %pad_maximum_fusion.1.local_ref, ...), custom_call_target="tpu_custom_call" | custom-call | flops 17179869184 | bytes 16777216 | tf_op jit(solution)/shard_map/pallas_call | solution.py:178
  155.1 1.9 multiply_bitcast_fusion.1.back_ref
  157.1 37.5 %shard_map.176 = bf16[32,512,512]{2,1,0:T(8,128)(2,1)} custom-call(bf16[32,512,512]{2,1,0:T(8,128)(2,1)} %u_ref.7, f32[16,64,512]{2,1,0:T(8,128)S(1)} %multiply_bitcast_fusion.1.back_ref, bf16[512,192]{1,0:T(8,128)(2,1)S(1)} %copy-done.10, bf16[2,256,256]{2,1,0:T(8,128)(2,1)S(1)} %pad_maximum_fusion.1.local_ref, ...), custom_call_target="tpu_custom_call", output_to_operand_aliasing={{}: (5, {})} | custom-call | flops 17179869184 | bytes 16777216 | tf_op jit(solution)/shard_map/pallas_call | solution.py:178
  (62 shorter events, 7.9 us)
Async XLA Ops:
  0.0 45.3 %copy-start = (f32[64,16]{0,1:T(8,128)S(1)}, f32[64,16]{0,1:T(8,128)}, u32[]{:S(2)}) copy-start(f32[64,16]{0,1:T(8,128)} %param.20) | copy-start | bytes 12292
  0.0 0.9 copy-start.4
  7.4 8.2 %copy-start.5 = (bf16[128,512]{1,0:T(8,128)(2,1)S(1)}, bf16[128,512]{1,0:T(8,128)(2,1)}, u32[]{:S(2)}) copy-start(bf16[128,512]{1,0:T(8,128)(2,1)} %constant.49.clone.basis_ref) | copy-start | bytes 393220
  9.1 31.4 %all-to-all-start.1 = ((f16[64,16,512]{2,1,0:T(8,128)(2,1)}), f16[64,16,512]{2,1,0:T(8,128)(2,1)S(1)}, u32[]{:S(2)}, u32[]{:S(2)}) async-start(f16[64,16,512]{2,1,0:T(8,128)(2,1)} %copy.62), calls=%async_computation.1 | async-start | bytes 2097152 | tf_op jit(solution)/shard_map/all_to_all | solution.py:235
  22.1 23.4 %copy-start.17 = (f32[16,16,16]{2,1,0:T(8,128)S(1)}, f32[16,16,16]{2,1,0:T(8,128)}, u32[]{:S(2)}) copy-start(f32[16,16,16]{2,1,0:T(8,128)} %param.22) | copy-start | bytes 49156
  22.2 23.5 %copy-start.15 = (f32[31,16,16]{2,1,0:T(8,128)S(1)}, f32[31,16,16]{2,1,0:T(8,128)}, u32[]{:S(2)}) copy-start(f32[31,16,16]{2,1,0:T(8,128)} %constant.60) | copy-start | bytes 95236
  22.2 23.5 %copy-start.16 = (f32[64,16,16]{0,2,1:T(8,128)S(1)}, f32[64,16,16]{0,2,1:T(8,128)}, u32[]{:S(2)}) copy-start(f32[64,16,16]{0,2,1:T(8,128)} %param.19) | copy-start | bytes 196612
  40.5 5.2 %copy-start.11 = (f16[64,16,512]{2,1,0:T(8,128)(2,1)}, f16[64,16,512]{2,1,0:T(8,128)(2,1)S(1)}, u32[]{:S(2)}) copy-start(f16[64,16,512]{2,1,0:T(8,128)(2,1)S(1)} %all-to-all-done.1) | copy-start | bytes 3145732
  40.5 29.8 %all-to-all-start = ((f16[64,16,512]{2,1,0:T(8,128)(2,1)}), f16[64,16,512]{2,1,0:T(8,128)(2,1)}, u32[]{:S(2)}, u32[]{:S(2)}) async-start(f16[64,16,512]{2,1,0:T(8,128)(2,1)} %copy.60), calls=%async_computation | async-start | bytes 2097152 | tf_op jit(solution)/shard_map/all_to_all | solution.py:235
  71.8 0.9 copy-start.6
  71.8 1.0 copy-start.7
  71.8 1.0 copy-start.8
  71.8 1.0 copy-start.9
  80.0 1.6 copy-start.2
  80.3 6.2 %copy-start.18 = (f32[16,16]{1,0:T(8,128)S(1)}, f32[16,16]{1,0:T(8,128)}, u32[]{:S(2)}) copy-start(f32[16,16]{1,0:T(8,128)} %param.21) | copy-start | bytes 3076
  81.6 29.7 %all-to-all-start.3 = ((f16[64,16,512]{2,1,0:T(8,128)(2,1)}), f16[64,16,512]{2,1,0:T(8,128)(2,1)S(1)}, u32[]{:S(2)}, u32[]{:S(2)}) async-start(f16[64,16,512]{2,1,0:T(8,128)(2,1)} %bitcast.27), calls=%async_computation.3 | async-start | bytes 2097152 | tf_op jit(solution)/shard_map/all_to_all | solution.py:264
  88.3 1.0 copy-start.19
  97.7 7.7 %copy-start.14 = (f32[256,16,16]{0,2,1:T(8,128)S(1)}, f32[256,16,16]{0,2,1:T(8,128)}, u32[]{:S(2)}) copy-start(f32[256,16,16]{0,2,1:T(8,128)} %constant.62) | copy-start | bytes 786436
  97.7 7.7 %copy-start.12 = (f32[256,512]{1,0:T(8,128)S(1)}, f32[256,512]{1,0:T(8,128)}, u32[]{:S(2)}) copy-start(f32[256,512]{1,0:T(8,128)} %constant.57.clone) | copy-start | bytes 1572868
  105.4 1.0 copy-start.13
  107.5 1.6 copy-start.3
  111.3 43.8 %all-to-all-start.2 = ((f16[64,16,512]{2,1,0:T(8,128)(2,1)}), f16[64,16,512]{2,1,0:T(8,128)(2,1)}, u32[]{:S(2)}, u32[]{:S(2)}) async-start(f16[64,16,512]{2,1,0:T(8,128)(2,1)} %bitcast.15), calls=%async_computation.2 | async-start | bytes 2097152 | tf_op jit(solution)/shard_map/all_to_all | solution.py:264
  116.7 0.9 copy-start.10
  157.1 37.5 %copy-start.1 = (f32[64,16]{0,1:T(8,128)S(1)}, f32[64,16]{0,1:T(8,128)}, u32[]{:S(2)}) copy-start(f32[64,16]{0,1:T(8,128)} %param.20) | copy-start | bytes 12292
